TPU v7x, 32 devices: a whole 2x2x4 slice. The times are simulated.
32 devices in a mesh: dp: 16 (over z, y, core), tensor: 2 (over x).
Axes of the slice: x: 2, y: 2, z: 4, core: 2. Of those that a mesh axis runs over, the one named last changes fastest.
Arguments:
- layer_input: bfloat16 [32768, 1024], P(('dp', 'tensor')), may hold values from -6 to 6
- target: bfloat16 [32768, 1024], P(('dp', 'tensor')), may hold values from -6 to 6
- segment: int32 [32768], P('dp'), may hold values from 0 to 2047, as said below
- pad_mask: int32 [32768], P(('dp', 'tensor')), may hold values from 0 to 1, as said below
- norm1_gain: float32 [1024], replicated, may hold values from 0.5 to 1.5
- w_query: bfloat16 [1024, 1024], P('dp', 'tensor'), may hold values from -0.1875 to 0.1875
- w_key: bfloat16 [1024, 1024], P('dp', 'tensor'), may hold values from -0.1875 to 0.1875
- w_value: bfloat16 [1024, 2048], P('dp', 'tensor'), may hold values from -0.1875 to 0.1875
- w_gate_out: bfloat16 [1024, 2048], P('dp', 'tensor'), may hold values from -0.1875 to 0.1875
- w_decay: bfloat16 [1024, 8], P('dp', 'tensor'), may hold values from -0.1875 to 0.1875
- w_beta: bfloat16 [1024, 8], P('dp', 'tensor'), may hold values from -0.1875 to 0.1875
- conv_query: float32 [4, 1024], replicated, may hold values from -3 to 3
- conv_key: float32 [4, 1024], replicated, may hold values from -3 to 3
- conv_value: float32 [4, 2048], replicated, may hold values from -3 to 3
- decay_scale: float32 [8], replicated, may hold values from 0.3 to 8
- decay_bias: float32 [8], replicated, may hold values from -5 to -2
- out_norm_gain: float32 [256], replicated, may hold values from 0.5 to 1.5
- w_out: bfloat16 [1024, 2048], P('dp', 'tensor'), may hold values from -0.25 to 0.25
- norm2_gain: float32 [1024], replicated, may hold values from 0.5 to 1.5
- w_ffn_gate: bfloat16 [1024, 2816], P('dp', 'tensor'), may hold values from -0.1875 to 0.1875
- w_ffn_up: bfloat16 [1024, 2816], P('dp', 'tensor'), may hold values from -0.1875 to 0.1875
- w_ffn_down: bfloat16 [1024, 2816], P('dp', 'tensor'), may hold values from -0.109375 to 0.109375
Outputs:
- output: float32 [32768, 1024], P(('dp', 'tensor'))
- loss: float32 [], replicated
- grad_input: float32 [32768, 1024], P(('dp', 'tensor'))
- grad_norm1_gain: float32 [1024], replicated
- grad_w_query: float32 [1024, 1024], P('dp', 'tensor')
- grad_w_key: float32 [1024, 1024], P('dp', 'tensor')
- grad_w_value: float32 [1024, 2048], P('dp', 'tensor')
- grad_w_gate_out: float32 [1024, 2048], P('dp', 'tensor')
- grad_w_decay: float32 [1024, 8], P('dp', 'tensor')
- grad_w_beta: float32 [1024, 8], P('dp', 'tensor')
- grad_conv_query: float32 [4, 1024], replicated
- grad_conv_key: float32 [4, 1024], replicated
- grad_conv_value: float32 [4, 2048], replicated
- grad_decay_scale: float32 [8], replicated
- grad_decay_bias: float32 [8], replicated
- grad_out_norm_gain: float32 [256], replicated
- grad_w_out: float32 [1024, 2048], P('dp', 'tensor')
- grad_norm2_gain: float32 [1024], replicated
- grad_w_ffn_gate: float32 [1024, 2816], P('dp', 'tensor')
- grad_w_ffn_up: float32 [1024, 2816], P('dp', 'tensor')
- grad_w_ffn_down: float32 [1024, 2816], P('dp', 'tensor')
Inputs may be any that keep to these rules, and one draw needn't show every extreme that they name: `segment`: ids never decrease within a sequence of 1024 tokens; each document's tokens share one id, the padding at a sequence's end has an id of its own, and different sequences share no id. Documents have 1 to 800 tokens, the last of a sequence cut to fit. `pad_mask`: each sequence of 1024 tokens ends with 1 to max(64, 2) padding tokens, marked 0; all other tokens are 1.
All inputs are finite; a program needn't handle non-finite values.
Results may differ from a plain program's by a relative error of at most 0.015.
Values may be sent and summed in bfloat16 or wider, within the bound.
No kernel may reach another device: no remote copies, remote signals or barrier semaphores. Data moves between devices by JAX's collectives and lax.ppermute only.
A program may use at most 384 MiB of HBM per device.

v0:
```python
import jax
import jax.numpy as jnp
from jax import lax
from jax.sharding import PartitionSpec as P

CH = 64
LENGTH = 1024
exact_precision = lax.Precision.HIGHEST


def rms_scale(values, gain):
    return values * lax.rsqrt(jnp.mean(values * values, axis=-1, keepdims=True) + 1e-06) * gain


def shift_masks(segment_ids, taps):
    masks = [jnp.ones(segment_ids.shape, jnp.float32)]
    for offset in range(1, taps):
        earlier = jnp.concatenate([jnp.full((offset,), -1, jnp.int32), segment_ids[:-offset]])
        masks.append((segment_ids == earlier).astype(jnp.float32))
    return masks


def short_conv(values, kernel, masks):
    result = values * kernel[0]
    for offset in range(1, len(masks)):
        shifted = jnp.concatenate(
            [jnp.zeros((offset, values.shape[1]), jnp.float32), values[:-offset]]
        )
        result = result + shifted * masks[offset][:, None] * kernel[offset]
    return result


def unit_rows(values):
    return values * lax.rsqrt(jnp.sum(values * values, axis=-1, keepdims=True) + 1e-06)


def lower_inverse(lower_part, length):
    negative = -lower_part
    inverse = jnp.eye(length, dtype=jnp.float32) + negative
    power = negative
    covered = 2
    while covered < length:
        power = jnp.einsum("hij,hjk->hik", power, power, precision=exact_precision)
        inverse = inverse + jnp.einsum("hij,hjk->hik", inverse, power, precision=exact_precision)
        covered = covered * 2
    return inverse


def block_update(state, inputs):
    queries, keys, values, betas, log_decay, seg_block, previous = inputs
    length = queries.shape[0]
    cumulative = jnp.cumsum(log_decay, axis=0)
    order = jnp.arange(length)
    causal = order[:, None] >= order[None, :]
    strict = order[:, None] > order[None, :]
    same_doc = seg_block[:, None] == seg_block[None, :]
    visible = (same_doc & causal)[:, :, None]
    spread = cumulative[:, None, :] - cumulative[None, :, :]
    weights = jnp.where(visible, jnp.exp(jnp.where(visible, spread, 0.0)), 0.0)
    carried = (seg_block == previous).astype(jnp.float32)
    carry_decay = jnp.exp(cumulative) * carried[:, None]
    key_gram = jnp.einsum("ihd,jhd->ijh", keys, keys, precision=exact_precision)
    lower_part = jnp.where(strict[:, :, None], betas[:, None, :] * weights * key_gram, 0.0)
    inverse = lower_inverse(jnp.transpose(lower_part, (2, 0, 1)), length)
    key_state = jnp.einsum("ihd,hde->ihe", keys, state, precision=exact_precision)
    target_rows = betas[:, :, None] * (values - carry_decay[:, :, None] * key_state)
    pseudo = jnp.einsum("hij,jhe->hie", inverse, target_rows, precision=exact_precision)
    scores = jnp.einsum("ihd,jhd->hij", queries, keys, precision=exact_precision) * jnp.transpose(
        weights, (2, 0, 1)
    )
    query_state = jnp.einsum("ihd,hde->ihe", queries, state, precision=exact_precision)
    outputs = carry_decay[:, :, None] * query_state + jnp.einsum(
        "hij,hje->ihe", scores, pseudo, precision=exact_precision
    )
    last_weights = weights[-1]
    new_state = (carried[-1] * jnp.exp(cumulative[-1]))[:, None, None] * state + jnp.einsum(
        "jh,jhd,hje->hde", last_weights, keys, pseudo, precision=exact_precision
    )
    return (new_state, outputs)


def mixer_sequence(
    q_pre,
    k_pre,
    v_pre,
    g_pre,
    a_pre,
    b_pre,
    segment_ids,
    conv_q,
    conv_k,
    conv_v,
    scale_rate,
    bias_rate,
    out_gain,
):
    length = q_pre.shape[0]
    heads = a_pre.shape[1]
    key_size = q_pre.shape[1] // heads
    value_size = v_pre.shape[1] // heads
    masks = shift_masks(segment_ids, conv_q.shape[0])
    queries = unit_rows(
        jax.nn.silu(short_conv(q_pre, conv_q, masks)).reshape(length, heads, key_size)
    ) * key_size ** (-0.5)
    keys = unit_rows(jax.nn.silu(short_conv(k_pre, conv_k, masks)).reshape(length, heads, key_size))
    values = jax.nn.silu(short_conv(v_pre, conv_v, masks)).reshape(length, heads, value_size)
    betas = jax.nn.sigmoid(b_pre)
    log_decay = -scale_rate * jax.nn.softplus(a_pre + bias_rate)
    blocks = length // CH
    seg_blocks = segment_ids.reshape(blocks, CH)
    previous = jnp.concatenate([jnp.full((1,), -1, jnp.int32), seg_blocks[:-1, -1]])
    state = jnp.zeros((heads, key_size, value_size), jnp.float32)
    carried_in = (
        queries.reshape(blocks, CH, heads, key_size),
        keys.reshape(blocks, CH, heads, key_size),
        values.reshape(blocks, CH, heads, value_size),
        betas.reshape(blocks, CH, heads),
        log_decay.reshape(blocks, CH, heads),
        seg_blocks,
        previous,
    )
    final_state, outputs = lax.scan(jax.checkpoint(block_update), state, carried_in)
    outputs = outputs.reshape(length, heads, value_size)
    gated = rms_scale(outputs, out_gain) * jax.nn.silu(g_pre.reshape(length, heads, value_size))
    return gated.reshape(length, heads * value_size)


def contract_rows(left, right):
    return lax.dot_general(
        left, right, (((0,), (0,)), ((), ())), preferred_element_type=jnp.float32
    )


def contract_cols(left, right):
    return lax.dot_general(
        left, right, (((1,), (1,)), ((), ())), preferred_element_type=jnp.float32
    )


def feed_inputs(normed_rows, gate_weight, up_weight):
    gate_pre = jnp.dot(normed_rows, gate_weight, preferred_element_type=jnp.float32)
    up_pre = jnp.dot(normed_rows, up_weight, preferred_element_type=jnp.float32)
    return (gate_pre, up_pre)


def on_device(
    layer_input,
    target,
    segment,
    pad_mask,
    norm1_gain,
    w_query,
    w_key,
    w_value,
    w_gate_out,
    w_decay,
    w_beta,
    conv_query,
    conv_key,
    conv_value,
    decay_scale,
    decay_bias,
    out_norm_gain,
    w_out,
    norm2_gain,
    w_ffn_gate,
    w_ffn_up,
    w_ffn_down,
):
    own_rows, width = layer_input.shape
    group_rows = segment.shape[0]
    sequences = group_rows // LENGTH
    tensor_index = lax.axis_index("tensor")
    heads_local = w_decay.shape[1]
    query_cols = w_query.shape[1]
    value_cols = w_value.shape[1]
    input_float = layer_input.astype(jnp.float32)
    normed_own, norm1_pull = jax.vjp(rms_scale, input_float, norm1_gain)
    normed = lax.all_gather(normed_own.astype(jnp.bfloat16), "tensor", axis=0, tiled=True)
    full_query, full_key, full_value, full_gate, full_decay, full_beta, full_out = (
        lax.all_gather(w_query, "dp", axis=0, tiled=True),
        lax.all_gather(w_key, "dp", axis=0, tiled=True),
        lax.all_gather(w_value, "dp", axis=0, tiled=True),
        lax.all_gather(w_gate_out, "dp", axis=0, tiled=True),
        lax.all_gather(w_decay, "dp", axis=0, tiled=True),
        lax.all_gather(w_beta, "dp", axis=0, tiled=True),
        lax.all_gather(w_out, "dp", axis=0, tiled=True),
    )
    proj_weights = (full_query, full_key, full_value, full_gate, full_decay, full_beta)
    projected = [
        jnp.dot(normed, weight, preferred_element_type=jnp.float32) for weight in proj_weights
    ]
    conv_q_local = lax.dynamic_slice_in_dim(conv_query, tensor_index * query_cols, query_cols, 1)
    conv_k_local = lax.dynamic_slice_in_dim(conv_key, tensor_index * query_cols, query_cols, 1)
    conv_v_local = lax.dynamic_slice_in_dim(conv_value, tensor_index * value_cols, value_cols, 1)
    scale_local = lax.dynamic_slice_in_dim(decay_scale, tensor_index * heads_local, heads_local, 0)
    bias_local = lax.dynamic_slice_in_dim(decay_bias, tensor_index * heads_local, heads_local, 0)
    seg_rows = segment.reshape(sequences, LENGTH)

    def mixer_local(
        q_pre,
        k_pre,
        v_pre,
        g_pre,
        a_pre,
        b_pre,
        conv_q,
        conv_k,
        conv_v,
        scale_rate,
        bias_rate,
        out_gain,
    ):
        shaped = [
            item.reshape(sequences, LENGTH, item.shape[1])
            for item in (q_pre, k_pre, v_pre, g_pre, a_pre, b_pre)
        ]
        mixed_rows = jax.vmap(
            mixer_sequence, in_axes=(0, 0, 0, 0, 0, 0, 0, None, None, None, None, None, None)
        )(*shaped, seg_rows, conv_q, conv_k, conv_v, scale_rate, bias_rate, out_gain)
        return mixed_rows.reshape(group_rows, mixed_rows.shape[2])

    mixed, mixer_pull = jax.vjp(
        mixer_local,
        *projected,
        conv_q_local,
        conv_k_local,
        conv_v_local,
        scale_local,
        bias_local,
        out_norm_gain
    )
    mixed_low = mixed.astype(jnp.bfloat16)
    attention = lax.psum_scatter(
        contract_cols(mixed_low, full_out), "tensor", scatter_dimension=0, tiled=True
    )
    residual = input_float + attention
    normed2_own, norm2_pull = jax.vjp(rms_scale, residual, norm2_gain)
    normed2 = lax.all_gather(normed2_own.astype(jnp.bfloat16), "tensor", axis=0, tiled=True)
    ffn_gate_w, ffn_up_w, ffn_down_w = (
        lax.all_gather(w_ffn_gate, "dp", axis=0, tiled=True),
        lax.all_gather(w_ffn_up, "dp", axis=0, tiled=True),
        lax.all_gather(w_ffn_down, "dp", axis=0, tiled=True),
    )
    gate_pre, up_pre = feed_inputs(normed2, ffn_gate_w, ffn_up_w)
    hidden = (jax.nn.silu(gate_pre) * up_pre).astype(jnp.bfloat16)
    ffn_out = lax.psum_scatter(
        contract_cols(hidden, ffn_down_w).astype(jnp.bfloat16),
        "tensor",
        scatter_dimension=0,
        tiled=True,
    ).astype(jnp.float32)
    output = residual + ffn_out
    live = pad_mask.astype(jnp.float32)
    error = output - target.astype(jnp.float32)
    loss_sum, count = lax.psum(
        (jnp.sum(live[:, None] * error * error), jnp.sum(live)), ("dp", "tensor")
    )
    loss = loss_sum / (count * width)
    all_tokens = own_rows * lax.axis_size("dp") * lax.axis_size("tensor")
    grad_output = error * live[:, None] * (all_tokens / count)
    grad_ffn = lax.all_gather(grad_output.astype(jnp.bfloat16), "tensor", axis=0, tiled=True)
    grad_hidden = jnp.dot(grad_ffn, ffn_down_w, preferred_element_type=jnp.float32)
    sigmoid_gate = jax.nn.sigmoid(gate_pre)
    grad_gate = (
        grad_hidden * up_pre * sigmoid_gate * (1.0 + gate_pre * (1.0 - sigmoid_gate))
    ).astype(jnp.bfloat16)
    grad_up = (grad_hidden * gate_pre * sigmoid_gate).astype(jnp.bfloat16)
    grad_down_local = contract_rows(grad_ffn, hidden)
    grad_gate_local = contract_rows(normed2, grad_gate)
    grad_up_local = contract_rows(normed2, grad_up)
    normed2_part = contract_cols(grad_gate, ffn_gate_w) + contract_cols(grad_up, ffn_up_w)
    grad_normed2 = lax.psum_scatter(
        normed2_part.astype(jnp.bfloat16), "tensor", scatter_dimension=0, tiled=True
    ).astype(jnp.float32)
    grad_residual_norm, grad_gain_two = norm2_pull(grad_normed2)
    grad_residual = grad_output + grad_residual_norm
    grad_attention = lax.all_gather(
        grad_residual.astype(jnp.bfloat16), "tensor", axis=0, tiled=True
    )
    grad_mixed = jnp.dot(grad_attention, full_out, preferred_element_type=jnp.float32)
    grad_out_local = contract_rows(grad_attention, mixed_low)
    mixer_grads = mixer_pull(grad_mixed)
    pre_grads = [item.astype(jnp.bfloat16) for item in mixer_grads[:6]]
    normed_part = contract_cols(pre_grads[0], full_query)
    for grad_item, weight in zip(pre_grads[1:], proj_weights[1:]):
        normed_part = normed_part + contract_cols(grad_item, weight)
    weight_locals = [contract_rows(normed, grad_item) for grad_item in pre_grads]
    grad_normed = lax.psum_scatter(
        normed_part.astype(jnp.bfloat16), "tensor", scatter_dimension=0, tiled=True
    ).astype(jnp.float32)
    grad_input_norm, grad_gain_one = norm1_pull(grad_normed)
    grad_input = grad_residual + grad_input_norm
    owned = (
        lax.psum_scatter(
            grad_gate_local.astype(jnp.bfloat16), "dp", scatter_dimension=0, tiled=True
        ).astype(jnp.float32),
        lax.psum_scatter(
            grad_up_local.astype(jnp.bfloat16), "dp", scatter_dimension=0, tiled=True
        ).astype(jnp.float32),
        lax.psum_scatter(
            grad_down_local.astype(jnp.bfloat16), "dp", scatter_dimension=0, tiled=True
        ).astype(jnp.float32),
        lax.psum_scatter(
            weight_locals[0].astype(jnp.bfloat16), "dp", scatter_dimension=0, tiled=True
        ).astype(jnp.float32),
        lax.psum_scatter(
            weight_locals[1].astype(jnp.bfloat16), "dp", scatter_dimension=0, tiled=True
        ).astype(jnp.float32),
        lax.psum_scatter(
            weight_locals[2].astype(jnp.bfloat16), "dp", scatter_dimension=0, tiled=True
        ).astype(jnp.float32),
        lax.psum_scatter(
            weight_locals[3].astype(jnp.bfloat16), "dp", scatter_dimension=0, tiled=True
        ).astype(jnp.float32),
        lax.psum_scatter(
            weight_locals[4].astype(jnp.bfloat16), "dp", scatter_dimension=0, tiled=True
        ).astype(jnp.float32),
        lax.psum_scatter(
            weight_locals[5].astype(jnp.bfloat16), "dp", scatter_dimension=0, tiled=True
        ).astype(jnp.float32),
        lax.psum_scatter(
            grad_out_local.astype(jnp.bfloat16), "dp", scatter_dimension=0, tiled=True
        ).astype(jnp.float32),
    )
    conv_q_full = lax.dynamic_update_slice_in_dim(
        jnp.zeros_like(conv_query), mixer_grads[6], tensor_index * query_cols, 1
    )
    conv_k_full = lax.dynamic_update_slice_in_dim(
        jnp.zeros_like(conv_key), mixer_grads[7], tensor_index * query_cols, 1
    )
    conv_v_full = lax.dynamic_update_slice_in_dim(
        jnp.zeros_like(conv_value), mixer_grads[8], tensor_index * value_cols, 1
    )
    scale_full = lax.dynamic_update_slice_in_dim(
        jnp.zeros_like(decay_scale), mixer_grads[9], tensor_index * heads_local, 0
    )
    bias_full = lax.dynamic_update_slice_in_dim(
        jnp.zeros_like(decay_bias), mixer_grads[10], tensor_index * heads_local, 0
    )
    summed = lax.psum(
        (
            grad_gain_one,
            grad_gain_two,
            conv_q_full,
            conv_k_full,
            conv_v_full,
            scale_full,
            bias_full,
            mixer_grads[11],
        ),
        ("dp", "tensor"),
    )
    return (
        output,
        loss,
        grad_input,
        summed[0],
        owned[3],
        owned[4],
        owned[5],
        owned[6],
        owned[7],
        owned[8],
        summed[2],
        summed[3],
        summed[4],
        summed[5],
        summed[6],
        summed[7],
        owned[9],
        summed[1],
        owned[0],
        owned[1],
        owned[2],
    )


def solution(mesh):
    return jax.shard_map(
        on_device,
        mesh=mesh,
        in_specs=(
            P(("dp", "tensor"), None),
            P(("dp", "tensor"), None),
            P("dp"),
            P(("dp", "tensor")),
            P(),
            P("dp", "tensor"),
            P("dp", "tensor"),
            P("dp", "tensor"),
            P("dp", "tensor"),
            P("dp", "tensor"),
            P("dp", "tensor"),
            P(),
            P(),
            P(),
            P(),
            P(),
            P(),
            P("dp", "tensor"),
            P(),
            P("dp", "tensor"),
            P("dp", "tensor"),
            P("dp", "tensor"),
        ),
        out_specs=(
            P(("dp", "tensor"), None),
            P(),
            P(("dp", "tensor"), None),
            P(),
            P("dp", "tensor"),
            P("dp", "tensor"),
            P("dp", "tensor"),
            P("dp", "tensor"),
            P("dp", "tensor"),
            P("dp", "tensor"),
            P(),
            P(),
            P(),
            P(),
            P(),
            P(),
            P("dp", "tensor"),
            P(),
            P("dp", "tensor"),
            P("dp", "tensor"),
            P("dp", "tensor"),
        ),
        check_vma=False,
    )
```

profile of v0, /device:TPU:0, one launch (start us, length us, event | category | flops | bytes accessed | tf_op | source)
XLA Modules:
  0.0 3118.4 jit_solution(9823898228020338124)
XLA Ops:
  17.5 23.1 all-gather
  40.8 17.4 all-gather.1
  60.5 48.3 %all-gather.15.cloned.1.call-done = bf16[2048,1024]{1,0:T(8,128)(2,1)} async-done(((bf16[1024,1024]{1,0:T(8,128)(2,1)}), bf16[2048,1024]{1,0:T(8,128)(2,1)}) %all-gather.15.cloned.1.call-update) | async-done | bytes 4194320 | tf_op jit(solution)/shard_map/all_gather | solution.py:179
  115.6 33.3 %all-gather.17.cloned.1.call-done = bf16[1024,512]{1,0:T(8,128)(2,1)} async-done(((bf16[64,512]{1,0:T(8,128)(2,1)}), bf16[1024,512]{1,0:T(8,128)(2,1)}) %all-gather.17.cloned.1.call-update) | async-done | bytes 1048592 | tf_op jit(solution)/shard_map/all_gather | solution.py:182
  154.0 9.3 fusion.200
  225.8 9.9 fusion.149
  235.7 10.6 reshape.641
  246.2 8.4 copy.457
  267.7 323.5 %while.42 = (s32[]{:T(128)}, f32[2,4,128,256]{3,2,1,0:T(8,128)S(1)}, f32[16,2,64,4,256]{4,2,3,1,0:T(8,128)}, f32[16,2,4,128,256]{4,3,2,1,0:T(8,128)}, s32[16,2,6...) while((s32[]{:T(128)}, ...), condition=%wide.region_5.6_spmd.clone, body=%wide.region_3.5_spmd.clone.sunk | while | flops 1160541952 | bytes 16545918 | solution.py:122
  604.9 13.8 copy.459
  618.6 8.8 copy.583
  627.4 18.5 multiply_convert_fusion.3
  645.9 10.8 fusion.230
  657.4 97.5 %reduce-scatter.19.cloned.1.call-done = f32[1024,1024]{1,0:T(8,128)} async-done(((f32[2048,1024]{1,0:T(8,128)}), f32[1024,1024]{1,0:T(8,128)}) %reduce-scatter.19.cloned.1.call-update) | async-done | bytes 4194320 | tf_op jit(solution)/shard_map/reduce_scatter | solution.py:234
  762.9 38.9 %all-gather.29.cloned.1.call-done = bf16[1024,1408]{1,0:T(8,128)(2,1)} async-done(((bf16[64,1408]{1,0:T(8,128)(2,1)}), bf16[1024,1408]{1,0:T(8,128)(2,1)}) %all-gather.29.cloned.1.call-update) | async-done | bytes 2883600 | tf_op jit(solution)/shard_map/all_gather | solution.py:241
  801.9 57.3 %all-gather.27.cloned.1.call-done = bf16[2048,1024]{1,0:T(8,128)(2,1)} async-done(((bf16[1024,1024]{1,0:T(8,128)(2,1)}), bf16[2048,1024]{1,0:T(8,128)(2,1)}) %all-gather.27.cloned.1.call-update) | async-done | bytes 4194320 | tf_op jit(solution)/shard_map/all_gather | solution.py:239
  859.2 11.9 fusion.231
  871.1 34.9 %all-gather.31.cloned.1.call-done = bf16[1024,1408]{1,0:T(8,128)(2,1)} async-done(((bf16[64,1408]{1,0:T(8,128)(2,1)}), bf16[1024,1408]{1,0:T(8,128)(2,1)}) %all-gather.31.cloned.1.call-update) | async-done | bytes 2883600 | tf_op jit(solution)/shard_map/all_gather | solution.py:242
  906.0 14.8 multiply_convert_fusion.2
  920.8 30.5 all-gather.33.cloned.1.call-done
  951.3 11.4 convolution_convert_fusion.3
  963.9 39.9 %psum.71 = f32[]{:T(128)} all-reduce(f32[]{:T(128)} %convert_reduce_fusion), channel_id=1, replica_groups=mesh['dp'=16,'tensor'=2] {'dp','tensor'}, use_global_device_ids=true, to_apply=%region_13.14 | all-reduce | flops 1 | bytes 8 | tf_op jit(solution)/shard_map/psum | solution.py:256
  1004.5 12.3 reduce-scatter.21.cloned.1.call-done
  1023.3 56.7 %all-gather.35.cloned.1.call-done = bf16[2048,1024]{1,0:T(8,128)(2,1)} async-done(((bf16[1024,1024]{1,0:T(8,128)(2,1)}), bf16[2048,1024]{1,0:T(8,128)(2,1)}) %all-gather.35.cloned.1.call-update) | async-done | bytes 4194320 | tf_op jit(solution)/shard_map/all_gather | solution.py:262
  1080.0 19.6 multiply_convert_fusion
  1099.6 8.9 fusion.232
  1108.6 8.4 add_convert_fusion.2
  1117.0 54.4 %reduce-scatter.23.cloned.1.call-done = bf16[1024,1024]{1,0:T(8,128)(2,1)} async-done(((bf16[2048,1024]{1,0:T(8,128)(2,1)}), bf16[1024,1024]{1,0:T(8,128)(2,1)}) %reduce-scatter.23.cloned.1.call-update) | async-done | bytes 2097168 | tf_op jit(solution)/shard_map/reduce_scatter | solution.py:273
  1183.9 11.9 convolution_convert_fusion
  1195.8 11.5 convolution_convert_fusion.2
  1209.4 10.6 reshape.647
  1229.4 11.5 convolution_convert_fusion.1
  1240.9 18.8 fusion.145
  1259.7 10.7 reshape.646
  1270.4 12.6 multiply_reduce_fusion.4
  1302.2 1161.9 %while.43 = (s32[]{:T(128)}, f32[2,4,128,256]{3,2,1,0:T(8,128)}, f32[16,2,64,4,128]{4,2,3,1,0:T(8,128)}, f32[16,2,64,4,128]{4,2,3,1,0:T(8,128)}, f32[16,2,64,4,2...) while((s32[]{:T(128)}, f32[2,4,128,256]{3,2,1,0:T(8,128)}, ...), condition=%wide.region_27.28_spmd.clone, body=%wide.region_17.27_spmd.clone.sunk | while | flops 3179373312 | bytes 74722920 | solution.py:122
  2534.9 28.9 multiply_reduce_fusion.18
  2593.6 13.9 copy.482
  2607.5 10.9 reshape.651
  2631.3 25.2 multiply_reduce_fusion.8
  2680.2 12.8 add_convert_fusion.1
  2739.2 16.4 add_convert_fusion
  2768.9 42.1 %reduce-scatter.27.cloned.1.call-done = bf16[64,512]{1,0:T(8,128)(2,1)} async-done(((bf16[1024,512]{1,0:T(8,128)(2,1)}), bf16[64,512]{1,0:T(8,128)(2,1)}) %reduce-scatter.27.cloned.1.call-update) | async-done | bytes 65552 | tf_op jit(solution)/shard_map/reduce_scatter | solution.py:304
  2812.6 62.8 %reduce-scatter.35.cloned.1.call-done = bf16[64,1024]{1,0:T(8,128)(2,1)} async-done(((bf16[1024,1024]{1,0:T(8,128)(2,1)}), bf16[64,1024]{1,0:T(8,128)(2,1)}) %reduce-scatter.35.cloned.1.call-update) | async-done | bytes 131088 | tf_op jit(solution)/shard_map/reduce_scatter | solution.py:322
  2877.0 63.1 %reduce-scatter.31.cloned.1.call-done = bf16[64,1024]{1,0:T(8,128)(2,1)} async-done(((bf16[1024,1024]{1,0:T(8,128)(2,1)}), bf16[64,1024]{1,0:T(8,128)(2,1)}) %reduce-scatter.31.cloned.1.call-update) | async-done | bytes 131088 | tf_op jit(solution)/shard_map/reduce_scatter | solution.py:310
  2941.6 62.7 %reduce-scatter.33.cloned.1.call-done = bf16[64,1024]{1,0:T(8,128)(2,1)} async-done(((bf16[1024,1024]{1,0:T(8,128)(2,1)}), bf16[64,1024]{1,0:T(8,128)(2,1)}) %reduce-scatter.33.cloned.1.call-update) | async-done | bytes 131088 | tf_op jit(solution)/shard_map/reduce_scatter | solution.py:313
  3005.9 54.5 %reduce-scatter.25.cloned.1.call-done = bf16[1024,1024]{1,0:T(8,128)(2,1)} async-done(((bf16[2048,1024]{1,0:T(8,128)(2,1)}), bf16[1024,1024]{1,0:T(8,128)(2,1)}) %reduce-scatter.25.cloned.1.call-update) | async-done | bytes 2097168 | tf_op jit(solution)/shard_map/reduce_scatter | solution.py:289
  3063.8 41.1 %all-reduce.38 = (f32[]{:T(128)}, f32[1024]{0:T(1024)}, f32[4,1024]{1,0:T(4,128)}, f32[4,1024]{1,0:T(4,128)}, f32[4,2048]{1,0:T(4,128)}, /*index=5*/f32[8]{0:T(128)}, f32[8]{0:T(128)}, f32[256]{0:T(256)}, f32[1024]{0:T(1024)}) all-reduce(f32[]{:T(128)} %get-tuple-element.925, ...), channel_id=1, replica_groups=mesh['dp'=16,'tensor'=2] {'dp','tensor'}, use_global_device_ids=true, to_apply=%region_11.12 | all-reduce | flops 18705 | bytes 149640 | tf_op jit(solution)/shard_map/psum | solution.py:256
  (3549 shorter events, 1825.8 us)
Async XLA Ops:
  7.2 53.3 %all-gather.21.cloned.1.call-start = ((), (), s32[]{:S(2)}) async-start(), calls=%async_computation.17 | async-start | bytes 1114112 | tf_op jit(solution)/shard_map/all_gather | solution.py:181
  8.0 100.7 %all-gather.15.cloned.1.call-start = ((), (), s32[]{:S(2)}) async-start(), calls=%async_computation.14 | async-start | bytes 6291456 | tf_op jit(solution)/shard_map/all_gather | solution.py:179
  14.8 134.1 %all-gather.17.cloned.1.call-start = ((), (), s32[]{:S(2)}) async-start(), calls=%async_computation.15 | async-start | bytes 1114112 | tf_op jit(solution)/shard_map/all_gather | solution.py:182
  15.6 203.2 %all-gather.19.cloned.1.call-start = ((), (), s32[]{:S(2)}) async-start(), calls=%async_computation.16 | async-start | bytes 2228224 | tf_op jit(solution)/shard_map/all_gather | solution.py:183
  16.1 611.3 %all-gather.23.cloned.1.call-start = ((), (), s32[]{:S(2)}) async-start(), calls=%async_computation.18 | async-start | bytes 2228224 | tf_op jit(solution)/shard_map/all_gather | solution.py:184
  16.7 629.1 %all-gather.25.cloned.1.call-start = ((), (), s32[]{:S(2)}) async-start(), calls=%async_computation.19 | async-start | bytes 2228224 | tf_op jit(solution)/shard_map/all_gather | solution.py:187
  17.3 737.6 %reduce-scatter.19.cloned.1.call-start = ((), (), s32[]{:S(2)}) async-start(), calls=%async_computation.20 | async-start | bytes 12582912 | tf_op jit(solution)/shard_map/reduce_scatter | solution.py:234
  40.7 213.9 %copy-start.89 = (bf16[1024,4]{0,1:T(4,128)(2,1)}, bf16[1024,4]{0,1:T(4,128)(2,1)S(1)}, u32[]{:S(2)}) copy-start(bf16[1024,4]{0,1:T(4,128)(2,1)S(1)} %reshape.655) | copy-start | bytes 24580
  40.8 221.0 %copy-start.128 = (f32[4]{0:T(128)}, f32[4]{0:T(128)S(1)}, u32[]{:S(2)}) copy-start(f32[4]{0:T(128)S(1)} %dynamic-slice_negate_fusion) | copy-start | bytes 52
  40.8 220.9 %copy-start.130 = (f32[4]{0:T(128)}, f32[4]{0:T(128)S(1)}, u32[]{:S(2)}) copy-start(f32[4]{0:T(128)S(1)} %dynamic_slice.145) | copy-start | bytes 52
  58.4 198.6 %copy-start.87 = (bf16[1024,4]{0,1:T(4,128)(2,1)}, bf16[1024,4]{0,1:T(4,128)(2,1)S(1)}, u32[]{:S(2)}) copy-start(bf16[1024,4]{0,1:T(4,128)(2,1)S(1)} %reshape.657) | copy-start | bytes 24580
  59.9 567.5 %copy-start.146 = (f32[1,2,4,128]{3,1,2,0:T(2,128)}, f32[1,2,4,128]{3,1,2,0:T(2,128)S(1)}, u32[]{:S(2)}) copy-start(f32[1,2,4,128]{3,1,2,0:T(2,128)S(1)} %copy.585) | copy-start | bytes 12292
  60.1 165.6 %copy-start.97 = (f32[1,1024]{1,0:T(1,128)}, f32[1,1024]{1,0:T(1,128)S(1)}, u32[]{:S(2)}) copy-start(f32[1,1024]{1,0:T(1,128)S(1)} %get-tuple-element.928) | copy-start | bytes 12292
  60.1 165.6 %copy-start.99 = (f32[1,1024]{1,0:T(1,128)}, f32[1,1024]{1,0:T(1,128)S(1)}, u32[]{:S(2)}) copy-start(f32[1,1024]{1,0:T(1,128)S(1)} %get-tuple-element.930) | copy-start | bytes 12292
  60.1 165.6 %copy-start.101 = (f32[1,1024]{1,0:T(1,128)}, f32[1,1024]{1,0:T(1,128)S(1)}, u32[]{:S(2)}) copy-start(f32[1,1024]{1,0:T(1,128)S(1)} %get-tuple-element.931) | copy-start | bytes 12292
  60.1 165.6 %copy-start.103 = (f32[1,1024]{1,0:T(1,128)}, f32[1,1024]{1,0:T(1,128)S(1)}, u32[]{:S(2)}) copy-start(f32[1,1024]{1,0:T(1,128)S(1)} %get-tuple-element.929) | copy-start | bytes 12292
  60.2 93.7 %copy-start.109 = (f32[1,512]{1,0:T(1,128)}, f32[1,512]{1,0:T(1,128)S(1)}, u32[]{:S(2)}) copy-start(f32[1,512]{1,0:T(1,128)S(1)} %get-tuple-element.960) | copy-start | bytes 6148
  60.2 93.7 %copy-start.111 = (f32[1,512]{1,0:T(1,128)}, f32[1,512]{1,0:T(1,128)S(1)}, u32[]{:S(2)}) copy-start(f32[1,512]{1,0:T(1,128)S(1)} %get-tuple-element.938) | copy-start | bytes 6148
  60.4 165.3 %copy-start.73 = (f32[2,1024]{1,0:T(2,128)}, f32[2,1024]{1,0:T(2,128)S(1)}, u32[]{:S(2)}) copy-start(f32[2,1024]{1,0:T(2,128)S(1)} %get-tuple-element.948) | copy-start | bytes 24580
  60.4 165.3 %copy-start.76 = (f32[2,1024]{1,0:T(2,128)}, f32[2,1024]{1,0:T(2,128)S(1)}, u32[]{:S(2)}) copy-start(f32[2,1024]{1,0:T(2,128)S(1)} %get-tuple-element.949) | copy-start | bytes 24580
  60.4 165.3 %copy-start.79 = (f32[2,1024]{1,0:T(2,128)}, f32[2,1024]{1,0:T(2,128)S(1)}, u32[]{:S(2)}) copy-start(f32[2,1024]{1,0:T(2,128)S(1)} %get-tuple-element.950) | copy-start | bytes 24580
  656.6 98.3 %copy-start.36 = (bf16[1024,1024]{1,0:T(8,128)(2,1)S(1)}, bf16[1024,1024]{1,0:T(8,128)(2,1)}, u32[]{:S(2)}) copy-start(bf16[1024,1024]{1,0:T(8,128)(2,1)} %param.26) | copy-start | bytes 6291460
  656.6 145.2 %all-gather.29.cloned.1.call-start = ((), (), s32[]{:S(2)}) async-start(), calls=%async_computation.22 | async-start | bytes 3063808 | tf_op jit(solution)/shard_map/all_gather | solution.py:241
  657.4 102.4 %copy-start.107 = (f32[1024]{0:T(1024)S(1)}, f32[1024]{0:T(1024)}, u32[]{:S(2)}) copy-start(f32[1024]{0:T(1024)} %param.44) | copy-start | bytes 12292
  657.4 201.8 %all-gather.27.cloned.1.call-start = ((), (), s32[]{:S(2)}) async-start(), calls=%async_computation.21 | async-start | bytes 6291456 | tf_op jit(solution)/shard_map/all_gather | solution.py:239
  761.6 144.4 %all-gather.31.cloned.1.call-start = ((), (), s32[]{:S(2)}) async-start(), calls=%async_computation.23 | async-start | bytes 3063808 | tf_op jit(solution)/shard_map/all_gather | solution.py:242
  762.2 189.1 %all-gather.33.cloned.1.call-start = ((), (), s32[]{:S(2)}) async-start(), calls=%async_computation.24 | async-start | bytes 3063808 | tf_op jit(solution)/shard_map/all_gather | solution.py:243
  762.9 253.9 %reduce-scatter.21.cloned.1.call-start = ((), (), s32[]{:S(2)}) async-start(), calls=%async_computation.25 | async-start | bytes 6291456 | tf_op jit(solution)/shard_map/reduce_scatter | solution.py:247
  962.6 117.4 %all-gather.35.cloned.1.call-start = ((), (), s32[]{:S(2)}) async-start(), calls=%async_computation.26 | async-start | bytes 6291456 | tf_op jit(solution)/shard_map/all_gather | solution.py:262
  1023.3 148.1 %reduce-scatter.23.cloned.1.call-start = ((), (), s32[]{:S(2)}) async-start(), calls=%async_computation.27 | async-start | bytes 6291456 | tf_op jit(solution)/shard_map/reduce_scatter | solution.py:273
  1116.9 124.0 %all-gather.37.cloned.1.call-start = ((), (), s32[]{:S(2)}) async-start(), calls=%async_computation.28 | async-start | bytes 6291456 | tf_op jit(solution)/shard_map/all_gather | solution.py:278
  1183.8 1572.7 %reduce-scatter.41.cloned.1.call-start = ((), (), s32[]{:S(2)}) async-start(), calls=%async_computation.37 | async-start | bytes 3063808 | tf_op jit(solution)/shard_map/reduce_scatter | solution.py:301
  1195.8 1562.6 %reduce-scatter.37.cloned.1.call-start = ((), (), s32[]{:S(2)}) async-start(), calls=%async_computation.35 | async-start | bytes 3063808 | tf_op jit(solution)/shard_map/reduce_scatter | solution.py:295
  1207.3 1552.7 %reduce-scatter.39.cloned.1.call-start = ((), (), s32[]{:S(2)}) async-start(), calls=%async_computation.36 | async-start | bytes 3063808 | tf_op jit(solution)/shard_map/reduce_scatter | solution.py:298
  1240.8 1523.8 %reduce-scatter.43.cloned.1.call-start = ((), (), s32[]{:S(2)}) async-start(), calls=%async_computation.38 | async-start | bytes 278528
  2576.3 189.7 %reduce-scatter.45.cloned.1.call-start = ((), (), s32[]{:S(2)}) async-start(), calls=%async_computation.39 | async-start | bytes 278528
  2580.1 187.3 %reduce-scatter.29.cloned.1.call-start = ((), (), s32[]{:S(2)}) async-start(), calls=%async_computation.31 | async-start | bytes 1114112 | tf_op jit(solution)/shard_map/reduce_scatter | solution.py:307
  2593.5 217.5 %reduce-scatter.27.cloned.1.call-start = ((), (), s32[]{:S(2)}) async-start(), calls=%async_computation.30 | async-start | bytes 1114112 | tf_op jit(solution)/shard_map/reduce_scatter | solution.py:304
  2631.2 244.1 %reduce-scatter.35.cloned.1.call-start = ((), (), s32[]{:S(2)}) async-start(), calls=%async_computation.34 | async-start | bytes 2228224 | tf_op jit(solution)/shard_map/reduce_scatter | solution.py:322
  2662.3 277.7 %reduce-scatter.31.cloned.1.call-start = ((), (), s32[]{:S(2)}) async-start(), calls=%async_computation.32 | async-start | bytes 2228224 | tf_op jit(solution)/shard_map/reduce_scatter | solution.py:310
  2700.9 303.4 %reduce-scatter.33.cloned.1.call-start = ((), (), s32[]{:S(2)}) async-start(), calls=%async_computation.33 | async-start | bytes 2228224 | tf_op jit(solution)/shard_map/reduce_scatter | solution.py:313
  2713.2 347.3 %reduce-scatter.25.cloned.1.call-start = ((), (), s32[]{:S(2)}) async-start(), calls=%async_computation.29 | async-start | bytes 6291456 | tf_op jit(solution)/shard_map/reduce_scatter | solution.py:289
  2755.7 304.8 %copy-start.37 = (bf16[1024,1024]{1,0:T(8,128)(2,1)S(1)}, bf16[1024,1024]{1,0:T(8,128)(2,1)}, u32[]{:S(2)}) copy-start(bf16[1024,1024]{1,0:T(8,128)(2,1)} %param.26) | copy-start | bytes 6291460
  2755.7 304.8 %copy-start.95 = (f32[1024]{0:T(1024)S(1)}, f32[1024]{0:T(1024)}, u32[]{:S(2)}) copy-start(f32[1024]{0:T(1024)} %copy-done.94) | copy-start | bytes 12292
  2755.7 304.8 %copy-start.96 = (f32[1024]{0:T(1024)S(1)}, f32[1024]{0:T(1024)}, u32[]{:S(2)}) copy-start(f32[1024]{0:T(1024)} %param.30) | copy-start | bytes 12292
  2760.0 303.8 %copy-start.106 = (f32[1024]{0:T(1024)S(1)}, f32[1024]{0:T(1024)}, u32[]{:S(2)}) copy-start(f32[1024]{0:T(1024)} %copy-done.105) | copy-start | bytes 12292
  2761.7 302.1 %copy-start.125 = (f32[1024]{0:T(1024)S(1)}, f32[1024]{0:T(1024)}, u32[]{:S(2)}) copy-start(f32[1024]{0:T(1024)} %get-tuple-element.798) | copy-start | bytes 12292
  2761.7 302.1 %copy-start.143 = (f32[256]{0:T(256)S(1)}, f32[256]{0:T(256)}, u32[]{:S(2)}) copy-start(f32[256]{0:T(256)} %get-tuple-element.792) | copy-start | bytes 3076
  (684 other events, 4767.5 us)
Sparse Core Ops, SparseCore 0:
  10.2 40.6 all-gather.20
  53.0 55.6 all-gather.14
  110.9 37.9 all-gather.16
  150.9 40.2 all-gather.18
  193.3 40.1 all-gather.22
  235.5 40.1 all-gather.24
  656.8 98.1 reduce-scatter.18
  757.5 44.3 all-gather.28
  804.1 55.0 all-gather.26
  861.6 44.3 all-gather.30
  908.5 42.6 all-gather.32
  962.8 54.0 reduce-scatter.20
  1023.4 56.5 all-gather.34
  1117.1 54.2 reduce-scatter.22
  1183.9 56.7 all-gather.36
  1244.8 65.0 reduce-scatter.40
  1313.6 63.9 reduce-scatter.36
  1381.8 63.8 reduce-scatter.38
  2576.4 55.6 reduce-scatter.42
  2636.1 54.2 reduce-scatter.44
  2694.0 56.4 reduce-scatter.28
  2754.5 56.4 reduce-scatter.26
  2814.8 60.4 reduce-scatter.34
  2879.4 60.5 reduce-scatter.30
  2943.8 60.5 reduce-scatter.32
  3007.1 53.2 reduce-scatter.24
where the time goes:
time: 3140 us; the launch traced here: 3120 us
  matrix products  1220 us (39%)
  waiting for transfers between devices  754 us (24%)
  local copies, waits for them, and re-layouts  576 us (18%)
  other arithmetic  386 us (12%)
  blocking collectives  122 us (4%)
  loops' own time  42.1 us (1%)
    dot_general x320, matrix products, lower_inverse(): power = jnp.einsum('hij,hjk->hik', power, power, precision=exact_precision)  163 us
    dot_general x320, matrix products, lower_inverse(): jnp.einsum('hij,hjk->hik', inverse, power, precision=exact_precision)  154 us
    squeeze x128, local copies, waits for them, and re-layouts, mixer_sequence(): lax.scan(jax.checkpoint(block_update), state, carried_in)  152 us
    dot_general x64, matrix products, block_update(): jnp.einsum('ihd,hde->ihe', keys, state, precision=exact_precision)  134 us
    dot_general x64, matrix products, block_update(): jnp.einsum('ihd,hde->ihe', queries, state, precision=exact_precision)  108 us
    reduce_scatter x1, waiting for transfers between devices, on_device(): lax.psum_scatter(contract_cols(mixed_low, full_out), 'tensor', scatter_di...  97.5 us
    dot_general x64, matrix products, block_update(): jnp.einsum('hij,jhe->hie', inverse, target_rows, precision=exact_precision)  91.9 us
    dot_general x10, matrix products, contract_cols(): lax.dot_general(left, right, (((1,), (1,)), ((), ())), preferred_element_...  87.2 us
  transfers between devices with their start and end apart: 26, of which 15 were waited for; matrix products, arithmetic and copies ran while one was open for 65% of the time, Pallas kernels for 0%

commit v1 on v0

--- a/solution.py
+++ b/solution.py
@@ -2,6 +2,7 @@
 import jax.numpy as jnp
 from jax import lax
 from jax.sharding import PartitionSpec as P
+from jax.lax import psum
 
 CH = 64
 LENGTH = 1024
@@ -167,6 +168,12 @@
     w_ffn_up,
     w_ffn_down,
 ):
+
+    def replace_figure(block_here, axis_id, row_axis="dp"):
+        block_now = psum(block_here, axis_id)
+        top = psum(block_now, row_axis)
+        return top
+
     own_rows, width = layer_input.shape
     group_rows = segment.shape[0]
     sequences = group_rows // LENGTH
@@ -253,8 +260,8 @@
     output = residual + ffn_out
     live = pad_mask.astype(jnp.float32)
     error = output - target.astype(jnp.float32)
-    loss_sum, count = lax.psum(
-        (jnp.sum(live[:, None] * error * error), jnp.sum(live)), ("dp", "tensor")
+    loss_sum, count = replace_figure(
+        (jnp.sum(live[:, None] * error * error), jnp.sum(live)), "tensor"
     )
     loss = loss_sum / (count * width)
     all_tokens = own_rows * lax.axis_size("dp") * lax.axis_size("tensor")

time: 3140 us -> 3270 us (1.041)
  waiting for transfers between devices: 754 us -> 910 us
  blocking collectives: 122 us -> 78.7 us
    psum x0 -> x1, waiting for transfers between devices: none -> 121 us  [on_device(): lax.psum((grad_gain_one, grad_gain_two, conv_q_full, conv_k_full, conv_v_...]
    psum x2, blocking collectives: 81 us -> 38.2 us  [the longest x1 32.6 us: replace_figure(): top = psum(block_now, row_axis)]
    reduce_scatter x1, waiting for transfers between devices: 12.3 us -> 51.5 us  [on_device(): lax.psum_scatter(contract_cols(hidden, ffn_down_w).astype(jnp.bfloat16),...]
  transfers between devices with their start and end apart: 26 -> 27, of which waited for: 15 -> 16; matrix products, arithmetic and copies ran while one was open for 65% -> 63% of each run, Pallas kernels for 0% -> 0%
where the time goes in v1:
time: 3270 us; the launch traced here: 3250 us
  matrix products  1220 us (37%)
  waiting for transfers between devices  910 us (28%)
  local copies, waits for them, and re-layouts  587 us (18%)
  other arithmetic  388 us (12%)
  blocking collectives  78.7 us (2%)
  loops' own time  42.1 us (1%)
    dot_general x320, matrix products, lower_inverse(): power = jnp.einsum('hij,hjk->hik', power, power, precision=exact_precision)  163 us
    dot_general x320, matrix products, lower_inverse(): jnp.einsum('hij,hjk->hik', inverse, power, precision=exact_precision)  154 us
    squeeze x128, local copies, waits for them, and re-layouts, mixer_sequence(): lax.scan(jax.checkpoint(block_update), state, carried_in)  152 us
    dot_general x64, matrix products, block_update(): jnp.einsum('ihd,hde->ihe', keys, state, precision=exact_precision)  134 us
    psum x1, waiting for transfers between devices, on_device(): lax.psum((grad_gain_one, grad_gain_two, conv_q_full, conv_k_full, conv_v_...  121 us
    dot_general x64, matrix products, block_update(): jnp.einsum('ihd,hde->ihe', queries, state, precision=exact_precision)  108 us
    reduce_scatter x1, waiting for transfers between devices, on_device(): lax.psum_scatter(contract_cols(mixed_low, full_out), 'tensor', scatter_di...  97.5 us
    dot_general x64, matrix products, block_update(): jnp.einsum('hij,jhe->hie', inverse, target_rows, precision=exact_precision)  91.8 us
  transfers between devices with their start and end apart: 27, of which 16 were waited for; matrix products, arithmetic and copies ran while one was open for 63% of the time, Pallas kernels for 0%

profile of v1, /device:TPU:0, one launch (start us, length us, event | category | flops | bytes accessed | tf_op | source)
XLA Modules:
  0.0 3245.8 jit_solution(7779879012395116374)
XLA Ops:
  17.5 23.1 all-gather
  40.8 17.4 all-gather.1
  60.5 48.3 %all-gather.15.cloned.1.call-done = bf16[2048,1024]{1,0:T(8,128)(2,1)} async-done(((bf16[1024,1024]{1,0:T(8,128)(2,1)}), bf16[2048,1024]{1,0:T(8,128)(2,1)}) %all-gather.15.cloned.1.call-update) | async-done | bytes 4194320 | tf_op jit(solution)/shard_map/all_gather | solution.py:186
  115.6 33.3 %all-gather.17.cloned.1.call-done = bf16[1024,512]{1,0:T(8,128)(2,1)} async-done(((bf16[64,512]{1,0:T(8,128)(2,1)}), bf16[1024,512]{1,0:T(8,128)(2,1)}) %all-gather.17.cloned.1.call-update) | async-done | bytes 1048592 | tf_op jit(solution)/shard_map/all_gather | solution.py:189
  154.0 9.3 fusion.200
  225.8 9.9 fusion.149
  235.8 10.5 reshape.641
  246.3 8.4 copy.457
  267.8 323.8 %while.42 = (s32[]{:T(128)}, f32[2,4,128,256]{3,2,1,0:T(8,128)S(1)}, f32[16,2,64,4,256]{4,2,3,1,0:T(8,128)}, f32[16,2,4,128,256]{4,3,2,1,0:T(8,128)}, s32[16,2,6...) while((s32[]{:T(128)}, ...), condition=%wide.region_5.6_spmd.clone, body=%wide.region_3.5_spmd.clone.sunk | while | flops 1160541952 | bytes 16545918 | solution.py:123
  605.3 13.8 copy.459
  619.0 8.7 copy.583
  627.8 18.5 multiply_convert_fusion.3
  646.3 10.8 fusion.230
  657.9 97.5 %reduce-scatter.19.cloned.1.call-done = f32[1024,1024]{1,0:T(8,128)} async-done(((f32[2048,1024]{1,0:T(8,128)}), f32[1024,1024]{1,0:T(8,128)}) %reduce-scatter.19.cloned.1.call-update) | async-done | bytes 4194320 | tf_op jit(solution)/shard_map/reduce_scatter | solution.py:241
  763.3 38.9 %all-gather.29.cloned.1.call-done = bf16[1024,1408]{1,0:T(8,128)(2,1)} async-done(((bf16[64,1408]{1,0:T(8,128)(2,1)}), bf16[1024,1408]{1,0:T(8,128)(2,1)}) %all-gather.29.cloned.1.call-update) | async-done | bytes 2883600 | tf_op jit(solution)/shard_map/all_gather | solution.py:248
  802.3 57.3 %all-gather.27.cloned.1.call-done = bf16[2048,1024]{1,0:T(8,128)(2,1)} async-done(((bf16[1024,1024]{1,0:T(8,128)(2,1)}), bf16[2048,1024]{1,0:T(8,128)(2,1)}) %all-gather.27.cloned.1.call-update) | async-done | bytes 4194320 | tf_op jit(solution)/shard_map/all_gather | solution.py:246
  859.6 11.9 fusion.231
  871.5 34.8 %all-gather.31.cloned.1.call-done = bf16[1024,1408]{1,0:T(8,128)(2,1)} async-done(((bf16[64,1408]{1,0:T(8,128)(2,1)}), bf16[1024,1408]{1,0:T(8,128)(2,1)}) %all-gather.31.cloned.1.call-update) | async-done | bytes 2883600 | tf_op jit(solution)/shard_map/all_gather | solution.py:249
  906.4 14.8 multiply_convert_fusion.2
  921.2 30.5 all-gather.33.cloned.1.call-done
  951.7 11.4 convolution_convert_fusion.3
  964.3 51.5 %reduce-scatter.21.cloned.1.call-done = bf16[1024,1024]{1,0:T(8,128)(2,1)} async-done(((bf16[2048,1024]{1,0:T(8,128)(2,1)}), bf16[1024,1024]{1,0:T(8,128)(2,1)}) %reduce-scatter.21.cloned.1.call-update) | async-done | bytes 2097168 | tf_op jit(solution)/shard_map/reduce_scatter | solution.py:254
  1027.7 32.6 %all-reduce.37 = (f32[]{:T(128)}, f32[]{:T(128)}) all-reduce(f32[]{:T(128)} %get-tuple-element.882, f32[]{:T(128)} %get-tuple-element.883), channel_id=1, replica_groups=mesh['dp'=16,'tensor'=2] {'dp'}, use_global_device_ids=true, to_apply=%region_12.13 | all-reduce | flops 2 | bytes 16 | tf_op jit(solution)/shard_map/psum | solution.py:174
  1065.2 53.2 %all-gather.35.cloned.1.call-done = bf16[2048,1024]{1,0:T(8,128)(2,1)} async-done(((bf16[1024,1024]{1,0:T(8,128)(2,1)}), bf16[2048,1024]{1,0:T(8,128)(2,1)}) %all-gather.35.cloned.1.call-update) | async-done | bytes 4194320 | tf_op jit(solution)/shard_map/all_gather | solution.py:269
  1118.4 19.6 multiply_convert_fusion
  1138.0 8.9 fusion.232
  1146.9 8.4 add_convert_fusion.2
  1155.4 54.4 %reduce-scatter.23.cloned.1.call-done = bf16[1024,1024]{1,0:T(8,128)(2,1)} async-done(((bf16[2048,1024]{1,0:T(8,128)(2,1)}), bf16[1024,1024]{1,0:T(8,128)(2,1)}) %reduce-scatter.23.cloned.1.call-update) | async-done | bytes 2097168 | tf_op jit(solution)/shard_map/reduce_scatter | solution.py:280
  1220.2 11.9 convolution_convert_fusion
  1232.2 11.5 convolution_convert_fusion.2
  1245.8 10.6 reshape.647
  1265.7 11.5 convolution_convert_fusion.1
  1277.3 18.8 fusion.145
  1296.0 10.7 reshape.646
  1306.7 12.6 multiply_reduce_fusion.4
  1338.5 1162.0 %while.43 = (s32[]{:T(128)}, f32[2,4,128,256]{3,2,1,0:T(8,128)}, f32[16,2,64,4,128]{4,2,3,1,0:T(8,128)}, f32[16,2,64,4,128]{4,2,3,1,0:T(8,128)}, f32[16,2,64,4,2...) while((s32[]{:T(128)}, f32[2,4,128,256]{3,2,1,0:T(8,128)}, ...), condition=%wide.region_29.30_spmd.clone, body=%wide.region_19.29_spmd.clone.sunk | while | flops 3179373312 | bytes 74722920 | solution.py:123
  2571.4 28.8 multiply_reduce_fusion.18
  2629.9 13.9 copy.482
  2643.9 10.9 reshape.651
  2667.7 25.0 multiply_reduce_fusion.8
  2716.5 12.8 add_convert_fusion.1
  2777.0 16.4 add_convert_fusion
  2807.4 40.1 %reduce-scatter.27.cloned.1.call-done = bf16[64,512]{1,0:T(8,128)(2,1)} async-done(((bf16[1024,512]{1,0:T(8,128)(2,1)}), bf16[64,512]{1,0:T(8,128)(2,1)}) %reduce-scatter.27.cloned.1.call-update) | async-done | bytes 65552 | tf_op jit(solution)/shard_map/reduce_scatter | solution.py:311
  2849.0 62.9 %reduce-scatter.35.cloned.1.call-done = bf16[64,1024]{1,0:T(8,128)(2,1)} async-done(((bf16[1024,1024]{1,0:T(8,128)(2,1)}), bf16[64,1024]{1,0:T(8,128)(2,1)}) %reduce-scatter.35.cloned.1.call-update) | async-done | bytes 131088 | tf_op jit(solution)/shard_map/reduce_scatter | solution.py:329
  2913.5 63.1 %reduce-scatter.31.cloned.1.call-done = bf16[64,1024]{1,0:T(8,128)(2,1)} async-done(((bf16[1024,1024]{1,0:T(8,128)(2,1)}), bf16[64,1024]{1,0:T(8,128)(2,1)}) %reduce-scatter.31.cloned.1.call-update) | async-done | bytes 131088 | tf_op jit(solution)/shard_map/reduce_scatter | solution.py:317
  2978.2 62.7 %reduce-scatter.33.cloned.1.call-done = bf16[64,1024]{1,0:T(8,128)(2,1)} async-done(((bf16[1024,1024]{1,0:T(8,128)(2,1)}), bf16[64,1024]{1,0:T(8,128)(2,1)}) %reduce-scatter.33.cloned.1.call-update) | async-done | bytes 131088 | tf_op jit(solution)/shard_map/reduce_scatter | solution.py:320
  3042.5 54.5 %reduce-scatter.25.cloned.1.call-done = bf16[1024,1024]{1,0:T(8,128)(2,1)} async-done(((bf16[2048,1024]{1,0:T(8,128)(2,1)}), bf16[1024,1024]{1,0:T(8,128)(2,1)}) %reduce-scatter.25.cloned.1.call-update) | async-done | bytes 2097168 | tf_op jit(solution)/shard_map/reduce_scatter | solution.py:296
  3105.8 121.4 %all-reduce.41.cloned.1.call-done = (f32[1024]{0:T(1024)}, f32[4,1024]{1,0:T(4,128)}, f32[4,1024]{1,0:T(4,128)}, f32[4,2048]{1,0:T(4,128)}, f32[8]{0:T(128)}, /*index=5*/f32[8]{0:T(128)}, f32[256]{0:T(256)}, f32[1024]{0:T(1024)}) async-done(((f32[1024]{0:T(1024)}, f32[4,1024]{1,0:T(4,128)}, f32[4,1024]{1,0:T(4,128)}, f32[4,2048]{1,0:T(4,128)}, f32[8]{0:T(128)}, /*index=5*/f32[8]{0:T(128)}, f32[256]{0:T(256)}, ...) | async-done | bytes 74832 | tf_op jit(solution)/shard_map/psum | solution.py:348
  (3565 shorter events, 1846.2 us)
Async XLA Ops:
  7.2 53.3 %all-gather.21.cloned.1.call-start = ((), (), s32[]{:S(2)}) async-start(), calls=%async_computation.17 | async-start | bytes 1114112 | tf_op jit(solution)/shard_map/all_gather | solution.py:188
  8.0 100.7 %all-gather.15.cloned.1.call-start = ((), (), s32[]{:S(2)}) async-start(), calls=%async_computation.14 | async-start | bytes 6291456 | tf_op jit(solution)/shard_map/all_gather | solution.py:186
  14.8 134.1 %all-gather.17.cloned.1.call-start = ((), (), s32[]{:S(2)}) async-start(), calls=%async_computation.15 | async-start | bytes 1114112 | tf_op jit(solution)/shard_map/all_gather | solution.py:189
  15.5 203.3 %all-gather.19.cloned.1.call-start = ((), (), s32[]{:S(2)}) async-start(), calls=%async_computation.16 | async-start | bytes 2228224 | tf_op jit(solution)/shard_map/all_gather | solution.py:190
  16.1 611.7 %all-gather.23.cloned.1.call-start = ((), (), s32[]{:S(2)}) async-start(), calls=%async_computation.18 | async-start | bytes 2228224 | tf_op jit(solution)/shard_map/all_gather | solution.py:191
  16.7 629.6 %all-gather.25.cloned.1.call-start = ((), (), s32[]{:S(2)}) async-start(), calls=%async_computation.19 | async-start | bytes 2228224 | tf_op jit(solution)/shard_map/all_gather | solution.py:194
  17.3 738.1 %reduce-scatter.19.cloned.1.call-start = ((), (), s32[]{:S(2)}) async-start(), calls=%async_computation.20 | async-start | bytes 12582912 | tf_op jit(solution)/shard_map/reduce_scatter | solution.py:241
  40.7 214.0 %copy-start.90 = (bf16[1024,4]{0,1:T(4,128)(2,1)}, bf16[1024,4]{0,1:T(4,128)(2,1)S(1)}, u32[]{:S(2)}) copy-start(bf16[1024,4]{0,1:T(4,128)(2,1)S(1)} %reshape.655) | copy-start | bytes 24580
  40.8 221.1 %copy-start.130 = (f32[4]{0:T(128)}, f32[4]{0:T(128)S(1)}, u32[]{:S(2)}) copy-start(f32[4]{0:T(128)S(1)} %dynamic-slice_negate_fusion) | copy-start | bytes 52
  40.8 221.0 %copy-start.132 = (f32[4]{0:T(128)}, f32[4]{0:T(128)S(1)}, u32[]{:S(2)}) copy-start(f32[4]{0:T(128)S(1)} %dynamic_slice.145) | copy-start | bytes 52
  58.4 198.6 %copy-start.88 = (bf16[1024,4]{0,1:T(4,128)(2,1)}, bf16[1024,4]{0,1:T(4,128)(2,1)S(1)}, u32[]{:S(2)}) copy-start(bf16[1024,4]{0,1:T(4,128)(2,1)S(1)} %reshape.657) | copy-start | bytes 24580
  59.9 567.9 %copy-start.147 = (f32[1,2,4,128]{3,1,2,0:T(2,128)}, f32[1,2,4,128]{3,1,2,0:T(2,128)S(1)}, u32[]{:S(2)}) copy-start(f32[1,2,4,128]{3,1,2,0:T(2,128)S(1)} %copy.585) | copy-start | bytes 12292
  60.1 165.7 %copy-start.101 = (f32[1,1024]{1,0:T(1,128)}, f32[1,1024]{1,0:T(1,128)S(1)}, u32[]{:S(2)}) copy-start(f32[1,1024]{1,0:T(1,128)S(1)} %get-tuple-element.930) | copy-start | bytes 12292
  60.1 165.7 %copy-start.103 = (f32[1,1024]{1,0:T(1,128)}, f32[1,1024]{1,0:T(1,128)S(1)}, u32[]{:S(2)}) copy-start(f32[1,1024]{1,0:T(1,128)S(1)} %get-tuple-element.932) | copy-start | bytes 12292
  60.1 165.7 %copy-start.105 = (f32[1,1024]{1,0:T(1,128)}, f32[1,1024]{1,0:T(1,128)S(1)}, u32[]{:S(2)}) copy-start(f32[1,1024]{1,0:T(1,128)S(1)} %get-tuple-element.933) | copy-start | bytes 12292
  60.1 165.7 %copy-start.107 = (f32[1,1024]{1,0:T(1,128)}, f32[1,1024]{1,0:T(1,128)S(1)}, u32[]{:S(2)}) copy-start(f32[1,1024]{1,0:T(1,128)S(1)} %get-tuple-element.931) | copy-start | bytes 12292
  60.4 165.4 %copy-start.73 = (f32[2,1024]{1,0:T(2,128)}, f32[2,1024]{1,0:T(2,128)S(1)}, u32[]{:S(2)}) copy-start(f32[2,1024]{1,0:T(2,128)S(1)} %get-tuple-element.950) | copy-start | bytes 24580
  60.4 165.4 %copy-start.76 = (f32[2,1024]{1,0:T(2,128)}, f32[2,1024]{1,0:T(2,128)S(1)}, u32[]{:S(2)}) copy-start(f32[2,1024]{1,0:T(2,128)S(1)} %get-tuple-element.951) | copy-start | bytes 24580
  60.4 165.4 %copy-start.79 = (f32[2,1024]{1,0:T(2,128)}, f32[2,1024]{1,0:T(2,128)S(1)}, u32[]{:S(2)}) copy-start(f32[2,1024]{1,0:T(2,128)S(1)} %get-tuple-element.952) | copy-start | bytes 24580
  657.1 145.2 %all-gather.29.cloned.1.call-start = ((), (), s32[]{:S(2)}) async-start(), calls=%async_computation.22 | async-start | bytes 3063808 | tf_op jit(solution)/shard_map/all_gather | solution.py:248
  657.8 201.8 %all-gather.27.cloned.1.call-start = ((), (), s32[]{:S(2)}) async-start(), calls=%async_computation.21 | async-start | bytes 6291456 | tf_op jit(solution)/shard_map/all_gather | solution.py:246
  762.0 144.4 %all-gather.31.cloned.1.call-start = ((), (), s32[]{:S(2)}) async-start(), calls=%async_computation.23 | async-start | bytes 3063808 | tf_op jit(solution)/shard_map/all_gather | solution.py:249
  762.6 189.1 %all-gather.33.cloned.1.call-start = ((), (), s32[]{:S(2)}) async-start(), calls=%async_computation.24 | async-start | bytes 3063808 | tf_op jit(solution)/shard_map/all_gather | solution.py:250
  763.3 252.5 %reduce-scatter.21.cloned.1.call-start = ((), (), s32[]{:S(2)}) async-start(), calls=%async_computation.25 | async-start | bytes 6291456 | tf_op jit(solution)/shard_map/reduce_scatter | solution.py:254
  963.1 155.3 %all-gather.35.cloned.1.call-start = ((), (), s32[]{:S(2)}) async-start(), calls=%async_computation.26 | async-start | bytes 6291456 | tf_op jit(solution)/shard_map/all_gather | solution.py:269
  1065.1 144.6 %reduce-scatter.23.cloned.1.call-start = ((), (), s32[]{:S(2)}) async-start(), calls=%async_computation.27 | async-start | bytes 6291456 | tf_op jit(solution)/shard_map/reduce_scatter | solution.py:280
  1155.3 121.9 %all-gather.37.cloned.1.call-start = ((), (), s32[]{:S(2)}) async-start(), calls=%async_computation.28 | async-start | bytes 6291456 | tf_op jit(solution)/shard_map/all_gather | solution.py:285
  1220.1 1575.0 %reduce-scatter.41.cloned.1.call-start = ((), (), s32[]{:S(2)}) async-start(), calls=%async_computation.37 | async-start | bytes 3063808 | tf_op jit(solution)/shard_map/reduce_scatter | solution.py:308
  1232.1 1564.7 %reduce-scatter.37.cloned.1.call-start = ((), (), s32[]{:S(2)}) async-start(), calls=%async_computation.35 | async-start | bytes 3063808 | tf_op jit(solution)/shard_map/reduce_scatter | solution.py:302
  1243.7 1554.8 %reduce-scatter.39.cloned.1.call-start = ((), (), s32[]{:S(2)}) async-start(), calls=%async_computation.36 | async-start | bytes 3063808 | tf_op jit(solution)/shard_map/reduce_scatter | solution.py:305
  1277.2 1526.0 %reduce-scatter.43.cloned.1.call-start = ((), (), s32[]{:S(2)}) async-start(), calls=%async_computation.38 | async-start | bytes 278528
  2612.7 191.8 %reduce-scatter.45.cloned.1.call-start = ((), (), s32[]{:S(2)}) async-start(), calls=%async_computation.39 | async-start | bytes 278528
  2616.5 189.4 %reduce-scatter.29.cloned.1.call-start = ((), (), s32[]{:S(2)}) async-start(), calls=%async_computation.31 | async-start | bytes 1114112 | tf_op jit(solution)/shard_map/reduce_scatter | solution.py:314
  2629.9 217.6 %reduce-scatter.27.cloned.1.call-start = ((), (), s32[]{:S(2)}) async-start(), calls=%async_computation.30 | async-start | bytes 1114112 | tf_op jit(solution)/shard_map/reduce_scatter | solution.py:311
  2667.6 244.3 %reduce-scatter.35.cloned.1.call-start = ((), (), s32[]{:S(2)}) async-start(), calls=%async_computation.34 | async-start | bytes 2228224 | tf_op jit(solution)/shard_map/reduce_scatter | solution.py:329
  2698.5 278.1 %reduce-scatter.31.cloned.1.call-start = ((), (), s32[]{:S(2)}) async-start(), calls=%async_computation.32 | async-start | bytes 2228224 | tf_op jit(solution)/shard_map/reduce_scatter | solution.py:317
  2737.2 303.7 %reduce-scatter.33.cloned.1.call-start = ((), (), s32[]{:S(2)}) async-start(), calls=%async_computation.33 | async-start | bytes 2228224 | tf_op jit(solution)/shard_map/reduce_scatter | solution.py:320
  2749.5 347.6 %reduce-scatter.25.cloned.1.call-start = ((), (), s32[]{:S(2)}) async-start(), calls=%async_computation.29 | async-start | bytes 6291456 | tf_op jit(solution)/shard_map/reduce_scatter | solution.py:296
  2793.5 303.6 %copy-start.37 = (bf16[1024,1024]{1,0:T(8,128)(2,1)S(1)}, bf16[1024,1024]{1,0:T(8,128)(2,1)}, u32[]{:S(2)}) copy-start(bf16[1024,1024]{1,0:T(8,128)(2,1)} %param.26) | copy-start | bytes 6291460
  2793.5 303.6 %copy-start.96 = (f32[1024]{0:T(1024)S(1)}, f32[1024]{0:T(1024)}, u32[]{:S(2)}) copy-start(f32[1024]{0:T(1024)} %copy-done.95) | copy-start | bytes 12292
  2793.5 303.6 %copy-start.100 = (f32[1024]{0:T(1024)S(1)}, f32[1024]{0:T(1024)}, u32[]{:S(2)}) copy-start(f32[1024]{0:T(1024)} %param.30) | copy-start | bytes 12292
  2793.5 433.6 %all-reduce.41.cloned.1.call-start = ((), (), s32[]{:S(2)}) async-start(), calls=%async_computation.40 | async-start | bytes 151552 | tf_op jit(solution)/shard_map/psum | solution.py:348
  2798.5 302.4 %copy-start.110 = (f32[1024]{0:T(1024)S(1)}, f32[1024]{0:T(1024)}, u32[]{:S(2)}) copy-start(f32[1024]{0:T(1024)} %copy-done.109) | copy-start | bytes 12292
  2802.8 298.2 %copy-start.152 = (f32[8]{0:T(128)}, f32[8]{0:T(128)S(1)}, u32[]{:S(2)}) copy-start(f32[8]{0:T(128)S(1)} %dynamic_update_slice.80) | copy-start | bytes 100
  2802.9 298.1 %copy-start.98 = (f32[4,1024]{1,0:T(4,128)}, f32[4,1024]{1,0:T(4,128)S(1)}, u32[]{:S(2)}) copy-start(f32[4,1024]{1,0:T(4,128)S(1)} %add_dynamic-update-slice_fusion.1) | copy-start | bytes 49156
  2803.0 298.1 %copy-start.97 = (f32[4,1024]{1,0:T(4,128)}, f32[4,1024]{1,0:T(4,128)S(1)}, u32[]{:S(2)}) copy-start(f32[4,1024]{1,0:T(4,128)S(1)} %add_dynamic-update-slice_fusion.2) | copy-start | bytes 49156
  2803.0 298.0 %copy-start.87 = (f32[4,2048]{1,0:T(4,128)}, f32[4,2048]{1,0:T(4,128)S(1)}, u32[]{:S(2)}) copy-start(f32[4,2048]{1,0:T(4,128)S(1)} %add_dynamic-update-slice_fusion) | copy-start | bytes 98308
  2803.1 297.9 %copy-start.151 = (f32[8]{0:T(128)}, f32[8]{0:T(128)S(1)}, u32[]{:S(2)}) copy-start(f32[8]{0:T(128)S(1)} %negate_dynamic-update-slice_fusion) | copy-start | bytes 100
  (687 other events, 5156.5 us)
Sparse Core Ops, SparseCore 0:
  10.2 40.6 all-gather.20
  53.0 55.6 all-gather.14
  110.9 37.9 all-gather.16
  150.9 40.3 all-gather.18
  193.3 40.1 all-gather.22
  235.5 40.2 all-gather.24
  657.2 98.1 reduce-scatter.18
  757.9 44.3 all-gather.28
  804.5 55.0 all-gather.26
  862.0 44.3 all-gather.30
  908.9 42.6 all-gather.32
  963.2 52.6 reduce-scatter.20
  1065.3 53.0 all-gather.34
  1155.5 54.2 reduce-scatter.22
  1220.2 56.7 all-gather.36
  1281.2 65.0 reduce-scatter.40
  1349.9 63.8 reduce-scatter.36
  1417.9 64.1 reduce-scatter.38
  2612.8 55.6 reduce-scatter.42
  2672.5 54.3 reduce-scatter.44
  2730.5 56.4 reduce-scatter.28
  2791.0 56.5 reduce-scatter.26
  2851.3 60.5 reduce-scatter.34
  2915.9 60.5 reduce-scatter.30
  2980.3 60.5 reduce-scatter.32
  3043.7 53.2 reduce-scatter.24
  3105.1 122.0 all-reduce.40
